TPU v7x, 32 devices: a whole 2x2x4 slice. The times are simulated.
32 devices in a mesh: dp: 16 (over z, y, x), mp: 2 (over core).
Axes of the slice: x: 2, y: 2, z: 4, core: 2. Of those that a mesh axis runs over, the one named last changes fastest.
Arguments:
- tokens: bfloat16 [32768, 768], P(('dp', 'mp')), may hold values from -6 to 6
- out_grad: bfloat16 [32768, 768], P(('dp', 'mp')), may hold values from -6 to 6
- image_lengths: int32 [16, 69], P('dp'), may hold values from 0 to 98, as said below
- group_of_block: int32 [16], P('dp'), may hold values from 0 to 2, as said below
- norm_gains: float32 [2, 768], replicated, may hold values from 0.5 to 1.5
- row_biases: float32 [4, 768], replicated, may hold values from -1.5 to 1.5
- w_qkv: bfloat16 [3, 768, 768], P(None, None, 'mp'), may hold values from -0.21875 to 0.21875
- qv_bias: float32 [2, 768], P(None, 'mp'), may hold values from -1.5 to 1.5
- w_out: bfloat16 [768, 768], P('mp'), may hold values from -0.875 to 0.875
- w_fc1: bfloat16 [768, 3072], P(None, 'mp'), may hold values from -0.21875 to 0.21875
- b_fc1: float32 [3072], P('mp'), may hold values from -1.5 to 1.5
- w_fc2: bfloat16 [3072, 768], P('mp'), may hold values from -0.109375 to 0.109375
Outputs:
- output: bfloat16 [32768, 768], P(('dp', 'mp'))
- tokens_grad: float32 [32768, 768], P(('dp', 'mp'))
- norm_gains_grad: float32 [2, 768], replicated
- row_biases_grad: float32 [4, 768], replicated
- w_qkv_grad: float32 [3, 768, 768], P(None, None, 'mp')
- qv_bias_grad: float32 [2, 768], P(None, 'mp')
- w_out_grad: float32 [768, 768], P('mp')
- w_fc1_grad: float32 [768, 3072], P(None, 'mp')
- b_fc1_grad: float32 [3072], P('mp')
- w_fc2_grad: float32 [3072, 768], P('mp')
Inputs may be any that keep to these rules, and one draw needn't show every extreme that they name: `image_lengths`: row b lists the patch counts of the images packed in block b from the first slot on; each image has 30 to 98 patches, slots after the last image hold 0, the counts of a row sum to at most 2048 and the rest of the block is padding; every block has an image of 98 patches. `group_of_block`: entry b is the dataset group of block b; it never falls along the blocks, and each of the 3 groups holds at least one block.
All inputs are finite; a program needn't handle non-finite values.
Results may differ from a plain program's by a relative error of at most 0.015.
Values may be sent and summed in bfloat16 or wider, within the bound.
No kernel may reach another device: no remote copies, remote signals or barrier semaphores. Data moves between devices by JAX's collectives and lax.ppermute only.
A program may use at most 256 MiB of HBM per device.

v0:
```python
import jax
import jax.numpy as jnp
from jax import lax
from jax.sharding import PartitionSpec as P

HEAD_DIM = 64
GROUPS = 3
LEN_NORM = 64


def layer_norm(values, gain_vec, shift_vec):
    center = values - jnp.mean(values, axis=-1, keepdims=True)
    spread = jnp.mean(center * center, axis=-1, keepdims=True)
    return center * lax.rsqrt(spread + 1e-06) * gain_vec + shift_vec


def gelu_tanh(values):
    return (
        0.5
        * values
        * (1.0 + jnp.tanh(0.7978845608028654 * (values + 0.044715 * values * values * values)))
    )


def image_rows(lengths, row_count):
    image_ends = jnp.cumsum(lengths)
    position = jnp.arange(row_count, dtype=jnp.int32)
    segment = jnp.sum((position[:, None] >= image_ends[None, :]).astype(jnp.int32), axis=1)
    slot_ids = jnp.arange(lengths.shape[0], dtype=jnp.int32)
    row_length = jnp.sum(
        jnp.where(segment[:, None] == slot_ids[None, :], lengths[None, :], 0), axis=1
    )
    return (segment, row_length)


def score_block(query_block, segment_block, keys_all, segment, score_scale):
    scores = (
        jnp.einsum("qhd,khd->hqk", query_block, keys_all, preferred_element_type=jnp.float32)
        * score_scale
    )
    return jnp.where((segment_block[:, None] == segment[None, :])[None], scores, -1000000000.0)


def local(
    tokens,
    out_grad,
    image_lengths,
    group_of_block,
    norm_gains,
    row_biases,
    w_qkv,
    qv_bias,
    w_out,
    w_fc1,
    b_fc1,
    w_fc2,
):
    own_rows = tokens.shape[0]
    row_count = own_rows * lax.axis_size("mp")
    first_row = lax.axis_index("mp") * own_rows
    segment, row_length = image_rows(image_lengths[0], row_count)
    images = jnp.sum((image_lengths[0] > 0).astype(jnp.float32))
    member = (group_of_block[0] == jnp.arange(GROUPS, dtype=jnp.int32)).astype(jnp.float32)
    group_images = lax.psum(member * images, "dp")
    group_roots = jnp.sqrt(group_images)
    factor = jnp.sum(group_images) / (group_roots * jnp.sum(group_roots))
    block_factor = jnp.sum(member * factor)
    own_length = lax.dynamic_slice_in_dim(row_length, first_row, own_rows)
    weight_row = (
        block_factor
        * LEN_NORM
        * (own_length > 0).astype(jnp.float32)
        / jnp.maximum(own_length, 1).astype(jnp.float32)
    )
    tokens_f = tokens.astype(jnp.float32)
    normed, norm_pull = jax.vjp(layer_norm, tokens_f, norm_gains[0], row_biases[0])
    normed_low = normed.astype(jnp.bfloat16)
    normed_all = lax.all_gather(normed_low, "mp", axis=0, tiled=True)
    projected = jnp.einsum("rd,tde->tre", normed_all, w_qkv, preferred_element_type=jnp.float32)
    bias_three = jnp.stack([qv_bias[0], jnp.zeros_like(qv_bias[0]), qv_bias[1]])
    projected = (projected + bias_three[:, None, :]).astype(jnp.bfloat16)
    local_width = w_qkv.shape[2]
    head_count = local_width // HEAD_DIM
    shaped = projected.reshape(3, row_count, head_count, HEAD_DIM)
    queries, keys_all, values_all = (shaped[0], shaped[1], shaped[2])
    block_rows = min(512, row_count)
    block_count = row_count // block_rows
    score_scale = HEAD_DIM ** (-0.5)
    query_blocks = queries.reshape(block_count, block_rows, head_count, HEAD_DIM)
    segment_blocks = segment.reshape(block_count, block_rows)

    def forward_block(pieces):
        query_block, segment_block = pieces
        scores = score_block(query_block, segment_block, keys_all, segment, score_scale)
        top_score = jnp.max(scores, axis=-1, keepdims=True)
        exponent = jnp.exp(scores - top_score)
        total = jnp.sum(exponent, axis=-1, keepdims=True)
        weights = (exponent / total).astype(jnp.bfloat16)
        context = jnp.einsum(
            "hqk,khd->qhd", weights, values_all, preferred_element_type=jnp.float32
        )
        return (context, (top_score + jnp.log(total))[:, :, 0])

    context, log_total = lax.map(forward_block, (query_blocks, segment_blocks))
    context_low = context.reshape(row_count, local_width).astype(jnp.bfloat16)
    piece = context_low
    attention = lax.psum_scatter(
        jnp.dot(piece, w_out, preferred_element_type=jnp.float32).astype(jnp.bfloat16),
        "mp",
        scatter_dimension=0,
        tiled=True,
    ).astype(jnp.float32)
    hidden_one = tokens_f + attention + row_biases[2]
    normed_two, norm_two_pull = jax.vjp(layer_norm, hidden_one, norm_gains[1], row_biases[1])
    normed_two_all = lax.all_gather(normed_two.astype(jnp.bfloat16), "mp", axis=0, tiled=True)
    before = jnp.dot(normed_two_all, w_fc1, preferred_element_type=jnp.float32) + b_fc1
    activated, gelu_pull = jax.vjp(gelu_tanh, before)
    activated_low = activated.astype(jnp.bfloat16)
    piece = activated_low
    mlp_out = lax.psum_scatter(
        jnp.dot(piece, w_fc2, preferred_element_type=jnp.float32).astype(jnp.bfloat16),
        "mp",
        scatter_dimension=0,
        tiled=True,
    ).astype(jnp.float32)
    output = (hidden_one + mlp_out + row_biases[3]).astype(jnp.bfloat16)
    out_cot = out_grad.astype(jnp.float32) * weight_row[:, None]
    out_cot_all = lax.all_gather(out_cot.astype(jnp.bfloat16), "mp", axis=0, tiled=True)
    grad_fc2 = jnp.einsum(
        "rf,rd->fd", activated_low, out_cot_all, preferred_element_type=jnp.float32
    )
    grad_act = jnp.einsum("rd,fd->rf", out_cot_all, w_fc2, preferred_element_type=jnp.float32)
    grad_before = gelu_pull(grad_act)[0].astype(jnp.bfloat16)
    grad_bfc1 = jnp.sum(grad_before.astype(jnp.float32), axis=0)
    grad_fc1 = jnp.einsum(
        "rd,rf->df", normed_two_all, grad_before, preferred_element_type=jnp.float32
    )
    piece = grad_before
    grad_norm_two = lax.psum_scatter(
        jnp.einsum("rf,df->rd", piece, w_fc1, preferred_element_type=jnp.float32).astype(
            jnp.bfloat16
        ),
        "mp",
        scatter_dimension=0,
        tiled=True,
    ).astype(jnp.float32)
    grad_hidden, grad_gain_two, grad_shift_two = norm_two_pull(grad_norm_two)
    grad_hidden = grad_hidden + out_cot
    grad_hidden_all = lax.all_gather(grad_hidden.astype(jnp.bfloat16), "mp", axis=0, tiled=True)
    grad_out = jnp.einsum(
        "rc,rd->cd", context_low, grad_hidden_all, preferred_element_type=jnp.float32
    )
    grad_context = jnp.einsum(
        "rd,cd->rc", grad_hidden_all, w_out, preferred_element_type=jnp.float32
    ).astype(jnp.bfloat16)
    context_blocks = grad_context.reshape(block_count, block_rows, head_count, HEAD_DIM)

    def backward_block(carry, pieces):
        grad_keys, grad_values = carry
        query_block, segment_block, log_block, grad_block = pieces
        scores = score_block(query_block, segment_block, keys_all, segment, score_scale)
        probs = jnp.exp(scores - log_block[:, :, None])
        grad_values = grad_values + jnp.einsum(
            "hqk,qhd->khd",
            probs.astype(jnp.bfloat16),
            grad_block,
            preferred_element_type=jnp.float32,
        )
        grad_probs = jnp.einsum(
            "qhd,khd->hqk", grad_block, values_all, preferred_element_type=jnp.float32
        )
        grad_scores = probs * (grad_probs - jnp.sum(probs * grad_probs, axis=-1, keepdims=True))
        grad_scores = grad_scores.astype(jnp.bfloat16)
        grad_query = (
            jnp.einsum("hqk,khd->qhd", grad_scores, keys_all, preferred_element_type=jnp.float32)
            * score_scale
        )
        grad_keys = (
            grad_keys
            + jnp.einsum(
                "hqk,qhd->khd", grad_scores, query_block, preferred_element_type=jnp.float32
            )
            * score_scale
        )
        return ((grad_keys, grad_values), grad_query)

    zero_heads = jnp.zeros((row_count, head_count, HEAD_DIM), jnp.float32)
    (grad_keys, grad_values), grad_queries = lax.scan(
        backward_block,
        (zero_heads, zero_heads),
        (query_blocks, segment_blocks, log_total, context_blocks),
    )
    grad_projected = jnp.stack(
        [
            grad_queries.reshape(row_count, local_width),
            grad_keys.reshape(row_count, local_width),
            grad_values.reshape(row_count, local_width),
        ]
    ).astype(jnp.bfloat16)
    grad_qv_bias = jnp.stack(
        [
            jnp.sum(grad_projected[0].astype(jnp.float32), axis=0),
            jnp.sum(grad_projected[2].astype(jnp.float32), axis=0),
        ]
    )
    grad_qkv = jnp.einsum(
        "rd,tre->tde", normed_all, grad_projected, preferred_element_type=jnp.float32
    )
    piece = grad_projected
    grad_norm_one = lax.psum_scatter(
        jnp.einsum("tre,tde->rd", piece, w_qkv, preferred_element_type=jnp.float32).astype(
            jnp.bfloat16
        ),
        "mp",
        scatter_dimension=0,
        tiled=True,
    ).astype(jnp.float32)
    grad_input, grad_gain_one, grad_shift_one = norm_pull(grad_norm_one)
    grad_input = grad_input + grad_hidden
    gain_grads, shift_grads = lax.psum(
        (
            jnp.stack([grad_gain_one, grad_gain_two]),
            jnp.stack(
                [
                    grad_shift_one,
                    grad_shift_two,
                    jnp.sum(grad_hidden, axis=0),
                    jnp.sum(out_cot, axis=0),
                ]
            ),
        ),
        ("dp", "mp"),
    )
    grad_qkv, grad_qv_bias, grad_out, grad_fc1, grad_bfc1, grad_fc2 = lax.psum(
        (grad_qkv, grad_qv_bias, grad_out, grad_fc1, grad_bfc1, grad_fc2), "dp"
    )
    return (
        output,
        grad_input,
        gain_grads,
        shift_grads,
        grad_qkv,
        grad_qv_bias,
        grad_out,
        grad_fc1,
        grad_bfc1,
        grad_fc2,
    )


def solution(mesh):
    placed = (
        P(("dp", "mp"), None),
        P(("dp", "mp"), None),
        P("dp", None),
        P("dp"),
        P(),
        P(),
        P(None, None, "mp"),
        P(None, "mp"),
        P("mp", None),
        P(None, "mp"),
        P("mp"),
        P("mp", None),
    )
    return jax.shard_map(
        local,
        mesh=mesh,
        in_specs=placed,
        out_specs=(
            P(("dp", "mp"), None),
            P(("dp", "mp"), None),
            P(),
            P(),
            P(None, None, "mp"),
            P(None, "mp"),
            P("mp", None),
            P(None, "mp"),
            P("mp"),
            P("mp", None),
        ),
        check_vma=False,
    )
```

profile of v0, /device:TPU:0, one launch (start us, length us, event | category | flops | bytes accessed | tf_op | source)
XLA Modules:
  0.0 1192.0 jit_solution(15143467741998065962)
XLA Ops:
  15.6 14.2 %all-gather.5.cloned.1.call-done = bf16[2048,768]{1,0:T(8,128)(2,1)} async-done(((bf16[1024,768]{1,0:T(8,128)(2,1)}), bf16[2048,768]{1,0:T(8,128)(2,1)}) %all-gather.5.cloned.1.call-update) | async-done | bytes 3145744 | tf_op jit(solution)/shard_map/all_gather | solution.py:78
  46.7 159.6 %while.27 = (s32[]{:T(128)}, bf16[4,512,6,64]{1,3,2,0:T(8,128)(2,1)}, f32[4,6,512]{2,1,0:T(8,128)S(1)}, s32[4,512]{1,0:T(4,128)S(1)}, s32[2048]{0:T(1024)S(1)}, ...) while((s32[]{:T(128)}, ...), condition=%wide.region_7.8_spmd, body=%wide.region_4.7_spmd.sunk | while | flops 1687155712 | bytes 103024832 | solution.py:104
  47.3 14.3 %fusion.128 = (f32[6,512]{1,0:T(8,128)S(1)}, f32[6,512,2048]{2,1,0:T(8,128)}) fusion(pred[512,2048]{1,0:T(8,128)(4,1)S(1)} %broadcast_compare_fusion.4, bf16[2048,6,64]{0,2,1:T(8,128)(2,1)} %get-tuple-element.469, bf16[4,512,6,64]{1,3,2,0:T(8,128)(2,1)} %get-tuple-element.468, s32[]{:T(128)S(6)} %copy.67), kind=kOutput, calls=%fused_computation.3.clone.1 | convolution fusion | flops 824177664 | bytes 28192772 | tf_op jit(solution)/shard_map/while/body/eval_jaxpr/qhd,khd->hqk/dot_general | solution.py:38
  61.6 12.1 %fusion.129 = f32[6,512]{1,0:T(8,128)S(1)} fusion(f32[6,512,2048]{2,1,0:T(8,128)} %get-tuple-element.430, f32[6,512]{1,0:T(8,128)S(1)} %get-tuple-element.431, pred[512,2048]{1,0:T(8,128)(4,1)S(1)} %broadcast_compare_fusion.4), kind=kLoop, calls=%fused_computation.4.clone.1 | loop fusion | flops 25162752 | bytes 26238976 | tf_op jit(solution)/shard_map/while/body/eval_jaxpr/reduce_sum | solution.py:97
  87.2 14.3 %fusion.128 = (f32[6,512]{1,0:T(8,128)S(1)}, f32[6,512,2048]{2,1,0:T(8,128)}) fusion(pred[512,2048]{1,0:T(8,128)(4,1)S(1)} %broadcast_compare_fusion.4, bf16[2048,6,64]{0,2,1:T(8,128)(2,1)} %get-tuple-element.469, bf16[4,512,6,64]{1,3,2,0:T(8,128)(2,1)} %get-tuple-element.468, s32[]{:T(128)S(6)} %copy.67), kind=kOutput, calls=%fused_computation.3.clone.1 | convolution fusion | flops 824177664 | bytes 28192772 | tf_op jit(solution)/shard_map/while/body/eval_jaxpr/qhd,khd->hqk/dot_general | solution.py:38
  101.5 12.1 %fusion.129 = f32[6,512]{1,0:T(8,128)S(1)} fusion(f32[6,512,2048]{2,1,0:T(8,128)} %get-tuple-element.430, f32[6,512]{1,0:T(8,128)S(1)} %get-tuple-element.431, pred[512,2048]{1,0:T(8,128)(4,1)S(1)} %broadcast_compare_fusion.4), kind=kLoop, calls=%fused_computation.4.clone.1 | loop fusion | flops 25162752 | bytes 26238976 | tf_op jit(solution)/shard_map/while/body/eval_jaxpr/reduce_sum | solution.py:97
  113.6 11.6 fusion.130
  127.1 14.3 %fusion.128 = (f32[6,512]{1,0:T(8,128)S(1)}, f32[6,512,2048]{2,1,0:T(8,128)}) fusion(pred[512,2048]{1,0:T(8,128)(4,1)S(1)} %broadcast_compare_fusion.4, bf16[2048,6,64]{0,2,1:T(8,128)(2,1)} %get-tuple-element.469, bf16[4,512,6,64]{1,3,2,0:T(8,128)(2,1)} %get-tuple-element.468, s32[]{:T(128)S(6)} %copy.67), kind=kOutput, calls=%fused_computation.3.clone.1 | convolution fusion | flops 824177664 | bytes 28192772 | tf_op jit(solution)/shard_map/while/body/eval_jaxpr/qhd,khd->hqk/dot_general | solution.py:38
  141.3 12.1 %fusion.129 = f32[6,512]{1,0:T(8,128)S(1)} fusion(f32[6,512,2048]{2,1,0:T(8,128)} %get-tuple-element.430, f32[6,512]{1,0:T(8,128)S(1)} %get-tuple-element.431, pred[512,2048]{1,0:T(8,128)(4,1)S(1)} %broadcast_compare_fusion.4), kind=kLoop, calls=%fused_computation.4.clone.1 | loop fusion | flops 25162752 | bytes 26238976 | tf_op jit(solution)/shard_map/while/body/eval_jaxpr/reduce_sum | solution.py:97
  166.9 14.3 %fusion.128 = (f32[6,512]{1,0:T(8,128)S(1)}, f32[6,512,2048]{2,1,0:T(8,128)}) fusion(pred[512,2048]{1,0:T(8,128)(4,1)S(1)} %broadcast_compare_fusion.4, bf16[2048,6,64]{0,2,1:T(8,128)(2,1)} %get-tuple-element.469, bf16[4,512,6,64]{1,3,2,0:T(8,128)(2,1)} %get-tuple-element.468, s32[]{:T(128)S(6)} %copy.67), kind=kOutput, calls=%fused_computation.3.clone.1 | convolution fusion | flops 824177664 | bytes 28192772 | tf_op jit(solution)/shard_map/while/body/eval_jaxpr/qhd,khd->hqk/dot_general | solution.py:38
  181.2 12.1 %fusion.129 = f32[6,512]{1,0:T(8,128)S(1)} fusion(f32[6,512,2048]{2,1,0:T(8,128)} %get-tuple-element.430, f32[6,512]{1,0:T(8,128)S(1)} %get-tuple-element.431, pred[512,2048]{1,0:T(8,128)(4,1)S(1)} %broadcast_compare_fusion.4), kind=kLoop, calls=%fused_computation.4.clone.1 | loop fusion | flops 25162752 | bytes 26238976 | tf_op jit(solution)/shard_map/while/body/eval_jaxpr/reduce_sum | solution.py:97
  214.2 12.2 %reduce-scatter.5.cloned.1.call-done = bf16[1024,768]{1,0:T(8,128)(2,1)} async-done(((bf16[2048,768]{1,0:T(8,128)(2,1)}), bf16[1024,768]{1,0:T(8,128)(2,1)}) %reduce-scatter.5.cloned.1.call-update) | async-done | bytes 1572880 | tf_op jit(solution)/shard_map/reduce_scatter | solution.py:107
  234.2 41.9 %psum.63 = f32[3]{0:T(128)S(1)} all-reduce(f32[3]{0:T(128)S(1)} %compare_select_fusion.1), channel_id=1, replica_groups=mesh['dp'=16,'mp'=2] {'dp'}, use_global_device_ids=true, to_apply=%region_14.15 | all-reduce | flops 3 | bytes 24 | tf_op jit(solution)/shard_map/psum | solution.py:64
  282.4 13.7 %multiply_convert_fusion.1 = (bf16[2048,1536]{1,0:T(8,128)(2,1)}, f32[2048,1536]{1,0:T(8,128)}) fusion(f32[1536]{0:T(1024)S(1)} %copy-done.48, bf16[2048,768]{1,0:T(8,128)(2,1)} %all-gather.7.cloned.1.call-done, bf16[768,1536]{1,0:T(8,128)(2,1)S(1)} %copy-done), kind=kOutput, calls=%fused_computation.58 | convolution fusion | flops 4863295488 | bytes 24385536 | tf_op jit(solution)/shard_map/dot_general | solution.py:116
  296.1 19.5 %convert_reduce_fusion = (f32[1536]{0:T(1024)}, bf16[2048,1536]{1,0:T(8,128)(2,1)S(1)}) fusion(bf16[2048,768]{1,0:T(8,128)(2,1)} %all-gather.9.cloned.1.call-done, bf16[1536,768]{1,0:T(8,128)(2,1)} %param.27, f32[2048,1536]{1,0:T(8,128)} %get-tuple-element.318, f32[1536]{0:T(1024)S(1)} %copy-done.48), kind=kOutput, calls=%fused_computation.57 | convolution fusion | flops 4916771328 | bytes 24391680 | tf_op jit(solution)/shard_map/rd,fd->rf/dot_general | solution.py:132
  355.0 13.4 %all-gather.11.cloned.1.call-done = bf16[2048,768]{1,0:T(8,128)(2,1)} async-done(((bf16[1024,768]{1,0:T(8,128)(2,1)}), bf16[2048,768]{1,0:T(8,128)(2,1)}) %all-gather.11.cloned.1.call-update) | async-done | bytes 3145744 | tf_op jit(solution)/shard_map/all_gather | solution.py:149
  381.7 333.3 %while.28 = (s32[]{:T(128)}, f32[2048,6,64]{0,2,1:T(8,128)}, f32[2048,6,64]{0,2,1:T(8,128)}, bf16[4,512,6,64]{1,3,2,0:T(8,128)(2,1)}, bf16[4,512,6,64]{1,3,2,0:T...) while((s32[]{:T(128)}, f32[2048,6,64]{0,2,1:T(8,128)}, ...), condition=%wide.region_23.24_spmd.clone, body=%wide.region_21.23_spmd.clone.sunk | while | flops 4126077952 | bytes 212699312 | solution.py:188
  393.7 12.8 %bitcast_add_fusion.5 = f32[2048,6,64]{0,2,1:T(8,128)} fusion(f32[2048,6,64]{0,2,1:T(8,128)} %get-tuple-element.487, f32[6,512,2048]{2,1,0:T(8,128)} %fusion.140, f32[6,512]{1,0:T(8,128)S(1)} %dynamic-slice_bitcast_fusion.2, pred[512,2048]{1,0:T(8,128)(4,1)S(1)} %broadcast_compare_fusion.5, pred[]{:T(512)S(6)} %compare.3, ...), kind=kOutput, calls=%fused_computation.23.clone.1 | convolution fusion | flops 832045056 | bytes 32911364 | tf_op jit(solution)/shard_map/while/body/eval_jaxpr/hqk,qhd->khd/dot_general | solution.py:163
  406.5 18.1 %multiply_reduce_fusion.3 = (f32[6,512]{1,0:T(8,128)S(1)}, f32[6,512,2048]{2,1,0:T(8,128)}) fusion(f32[6,512,2048]{2,1,0:T(8,128)} %fusion.140, f32[6,512]{1,0:T(8,128)S(1)} %dynamic-slice_bitcast_fusion.2, pred[512,2048]{1,0:T(8,128)(4,1)S(1)} %broadcast_compare_fusion.5, bf16[2048,6,64]{0,2,1:T(8,128)(2,1)} %get-tuple-element.508, ...), kind=kOutput, calls=%fused_computation.18.clone.1 | convolution fusion | flops 836760576 | bytes 53370884 | tf_op jit(solution)/shard_map/while/body/eval_jaxpr/qhd,khd->hqk/dot_general | solution.py:169
  424.6 21.3 %multiply_convert_fusion.3 = bf16[6,512,2048]{2,1,0:T(8,128)(2,1)} fusion(f32[6,512,2048]{2,1,0:T(8,128)} %get-tuple-element.443, f32[6,512,2048]{2,1,0:T(8,128)} %fusion.140, f32[6,512]{1,0:T(8,128)S(1)} %get-tuple-element.444, f32[6,512]{1,0:T(8,128)S(1)} %dynamic-slice_bitcast_fusion.2, pred[512,2048]{1,0:T(8,128)(4,1)S(1)} %broadcast_compare_fusion.5), kind=kLoop, calls=%fused_computation.17.clone.1 | loop fusion | flops 37748736 | bytes 63987712 | tf_op jit(solution)/shard_map/while/body/eval_jaxpr/convert_element_type | solution.py:173
  475.5 13.7 %bitcast_add_fusion.5 = f32[2048,6,64]{0,2,1:T(8,128)} fusion(f32[2048,6,64]{0,2,1:T(8,128)} %get-tuple-element.487, f32[6,512,2048]{2,1,0:T(8,128)} %fusion.140, f32[6,512]{1,0:T(8,128)S(1)} %dynamic-slice_bitcast_fusion.2, pred[512,2048]{1,0:T(8,128)(4,1)S(1)} %broadcast_compare_fusion.5, pred[]{:T(512)S(6)} %compare.3, ...), kind=kOutput, calls=%fused_computation.23.clone.1 | convolution fusion | flops 832045056 | bytes 32911364 | tf_op jit(solution)/shard_map/while/body/eval_jaxpr/hqk,qhd->khd/dot_general | solution.py:163
  489.2 18.1 %multiply_reduce_fusion.3 = (f32[6,512]{1,0:T(8,128)S(1)}, f32[6,512,2048]{2,1,0:T(8,128)}) fusion(f32[6,512,2048]{2,1,0:T(8,128)} %fusion.140, f32[6,512]{1,0:T(8,128)S(1)} %dynamic-slice_bitcast_fusion.2, pred[512,2048]{1,0:T(8,128)(4,1)S(1)} %broadcast_compare_fusion.5, bf16[2048,6,64]{0,2,1:T(8,128)(2,1)} %get-tuple-element.508, ...), kind=kOutput, calls=%fused_computation.18.clone.1 | convolution fusion | flops 836760576 | bytes 53370884 | tf_op jit(solution)/shard_map/while/body/eval_jaxpr/qhd,khd->hqk/dot_general | solution.py:169
  507.3 21.3 %multiply_convert_fusion.3 = bf16[6,512,2048]{2,1,0:T(8,128)(2,1)} fusion(f32[6,512,2048]{2,1,0:T(8,128)} %get-tuple-element.443, f32[6,512,2048]{2,1,0:T(8,128)} %fusion.140, f32[6,512]{1,0:T(8,128)S(1)} %get-tuple-element.444, f32[6,512]{1,0:T(8,128)S(1)} %dynamic-slice_bitcast_fusion.2, pred[512,2048]{1,0:T(8,128)(4,1)S(1)} %broadcast_compare_fusion.5), kind=kLoop, calls=%fused_computation.17.clone.1 | loop fusion | flops 37748736 | bytes 63987712 | tf_op jit(solution)/shard_map/while/body/eval_jaxpr/convert_element_type | solution.py:173
  559.1 13.7 %bitcast_add_fusion.5 = f32[2048,6,64]{0,2,1:T(8,128)} fusion(f32[2048,6,64]{0,2,1:T(8,128)} %get-tuple-element.487, f32[6,512,2048]{2,1,0:T(8,128)} %fusion.140, f32[6,512]{1,0:T(8,128)S(1)} %dynamic-slice_bitcast_fusion.2, pred[512,2048]{1,0:T(8,128)(4,1)S(1)} %broadcast_compare_fusion.5, pred[]{:T(512)S(6)} %compare.3, ...), kind=kOutput, calls=%fused_computation.23.clone.1 | convolution fusion | flops 832045056 | bytes 32911364 | tf_op jit(solution)/shard_map/while/body/eval_jaxpr/hqk,qhd->khd/dot_general | solution.py:163
  572.8 18.1 %multiply_reduce_fusion.3 = (f32[6,512]{1,0:T(8,128)S(1)}, f32[6,512,2048]{2,1,0:T(8,128)}) fusion(f32[6,512,2048]{2,1,0:T(8,128)} %fusion.140, f32[6,512]{1,0:T(8,128)S(1)} %dynamic-slice_bitcast_fusion.2, pred[512,2048]{1,0:T(8,128)(4,1)S(1)} %broadcast_compare_fusion.5, bf16[2048,6,64]{0,2,1:T(8,128)(2,1)} %get-tuple-element.508, ...), kind=kOutput, calls=%fused_computation.18.clone.1 | convolution fusion | flops 836760576 | bytes 53370884 | tf_op jit(solution)/shard_map/while/body/eval_jaxpr/qhd,khd->hqk/dot_general | solution.py:169
  590.9 21.3 %multiply_convert_fusion.3 = bf16[6,512,2048]{2,1,0:T(8,128)(2,1)} fusion(f32[6,512,2048]{2,1,0:T(8,128)} %get-tuple-element.443, f32[6,512,2048]{2,1,0:T(8,128)} %fusion.140, f32[6,512]{1,0:T(8,128)S(1)} %get-tuple-element.444, f32[6,512]{1,0:T(8,128)S(1)} %dynamic-slice_bitcast_fusion.2, pred[512,2048]{1,0:T(8,128)(4,1)S(1)} %broadcast_compare_fusion.5), kind=kLoop, calls=%fused_computation.17.clone.1 | loop fusion | flops 37748736 | bytes 63987712 | tf_op jit(solution)/shard_map/while/body/eval_jaxpr/convert_element_type | solution.py:173
  642.7 13.7 %bitcast_add_fusion.5 = f32[2048,6,64]{0,2,1:T(8,128)} fusion(f32[2048,6,64]{0,2,1:T(8,128)} %get-tuple-element.487, f32[6,512,2048]{2,1,0:T(8,128)} %fusion.140, f32[6,512]{1,0:T(8,128)S(1)} %dynamic-slice_bitcast_fusion.2, pred[512,2048]{1,0:T(8,128)(4,1)S(1)} %broadcast_compare_fusion.5, pred[]{:T(512)S(6)} %compare.3, ...), kind=kOutput, calls=%fused_computation.23.clone.1 | convolution fusion | flops 832045056 | bytes 32911364 | tf_op jit(solution)/shard_map/while/body/eval_jaxpr/hqk,qhd->khd/dot_general | solution.py:163
  656.4 18.1 %multiply_reduce_fusion.3 = (f32[6,512]{1,0:T(8,128)S(1)}, f32[6,512,2048]{2,1,0:T(8,128)}) fusion(f32[6,512,2048]{2,1,0:T(8,128)} %fusion.140, f32[6,512]{1,0:T(8,128)S(1)} %dynamic-slice_bitcast_fusion.2, pred[512,2048]{1,0:T(8,128)(4,1)S(1)} %broadcast_compare_fusion.5, bf16[2048,6,64]{0,2,1:T(8,128)(2,1)} %get-tuple-element.508, ...), kind=kOutput, calls=%fused_computation.18.clone.1 | convolution fusion | flops 836760576 | bytes 53370884 | tf_op jit(solution)/shard_map/while/body/eval_jaxpr/qhd,khd->hqk/dot_general | solution.py:169
  674.5 21.3 %multiply_convert_fusion.3 = bf16[6,512,2048]{2,1,0:T(8,128)(2,1)} fusion(f32[6,512,2048]{2,1,0:T(8,128)} %get-tuple-element.443, f32[6,512,2048]{2,1,0:T(8,128)} %fusion.140, f32[6,512]{1,0:T(8,128)S(1)} %get-tuple-element.444, f32[6,512]{1,0:T(8,128)S(1)} %dynamic-slice_bitcast_fusion.2, pred[512,2048]{1,0:T(8,128)(4,1)S(1)} %broadcast_compare_fusion.5), kind=kLoop, calls=%fused_computation.17.clone.1 | loop fusion | flops 37748736 | bytes 63987712 | tf_op jit(solution)/shard_map/while/body/eval_jaxpr/convert_element_type | solution.py:173
  772.7 81.2 %all-reduce.1 = (f32[2,384]{1,0:T(2,128)}, f32[1536]{0:T(1024)}) all-reduce(f32[2,384]{1,0:T(2,128)S(1)} %pad_maximum_fusion.6, f32[1536]{0:T(1024)S(1)} %copy-done.38), channel_id=1, replica_groups=mesh['dp'=16,'mp'=2] {'dp'}, use_global_device_ids=true, to_apply=%region_38.39 | all-reduce | flops 2304 | bytes 18432 | tf_op jit(solution)/shard_map/psum | solution.py:234
  858.7 41.5 %all-reduce = (f32[2,768]{1,0:T(2,128)}, f32[4,768]{1,0:T(4,128)}) all-reduce(f32[2,768]{1,0:T(2,128)S(1)} %pad_maximum_fusion.5, f32[4,768]{1,0:T(4,128)S(1)} %pad_maximum_fusion.3), channel_id=1, replica_groups=mesh['dp'=16,'mp'=2] {'dp','mp'}, use_global_device_ids=true, to_apply=%region_29.30 | all-reduce | flops 4608 | bytes 36864 | tf_op jit(solution)/shard_map/psum | solution.py:220
  904.2 267.0 %all-reduce.5.cloned.1.call-done = (f32[3,768,384]{1,2,0:T(8,128)}, f32[384,768]{1,0:T(8,128)}, f32[768,1536]{1,0:T(8,128)}, f32[1536,768]{1,0:T(8,128)}) async-done(((f32[3,768,384]{1,2,0:T(8,128)}, f32[384,768]{1,0:T(8,128)}, f32[768,1536]{1,0:T(8,128)}, f32[1536,768]{1,0:T(8,128)}), (f32[3,768,384]{1,2,0:T(8,128)}, f32[384,768]{1,0:T(8,128)}, f32[768,1536]{1,0:T(8,128)}, ...) | async-done | bytes 14155792 | tf_op jit(solution)/shard_map/psum | solution.py:234
  (269 shorter events, 342.1 us)
Async XLA Ops:
  7.2 275.3 %copy-start = (bf16[768,1536]{1,0:T(8,128)(2,1)S(1)}, bf16[768,1536]{1,0:T(8,128)(2,1)}, u32[]{:S(2)}) copy-start(bf16[768,1536]{1,0:T(8,128)(2,1)} %param.25) | copy-start | bytes 7077892
  7.2 22.6 %all-gather.5.cloned.1.call-start = ((), (), s32[]{:S(2)}) async-start(), calls=%async_computation.4 | async-start | bytes 4718592 | tf_op jit(solution)/shard_map/all_gather | solution.py:78
  9.1 5.8 copy-start.41
  9.1 6.3 copy-start.40
  14.8 211.6 %reduce-scatter.5.cloned.1.call-start = ((), (), s32[]{:S(2)}) async-start(), calls=%async_computation.5 | async-start | bytes 4718592 | tf_op jit(solution)/shard_map/reduce_scatter | solution.py:107
  61.6 12.1 %copy-start.7 = (bf16[2048,6,64]{0,2,1:T(8,128)(2,1)S(1)}, bf16[2048,6,64]{0,2,1:T(8,128)(2,1)}, u32[]{:S(2)}) copy-start(bf16[2048,6,64]{0,2,1:T(8,128)(2,1)} %get-tuple-element.470) | copy-start | bytes 4718596 | tf_op jit(solution)/shard_map/while
  61.6 12.1 %copy-start.13 = (bf16[4,512,6,64]{1,3,2,0:T(8,128)(2,1)S(1)}, bf16[4,512,6,64]{1,3,2,0:T(8,128)(2,1)}, u32[]{:S(2)}) copy-start(bf16[4,512,6,64]{1,3,2,0:T(8,128)(2,1)} %get-tuple-element.455) | copy-start | bytes 4718596 | tf_op jit(solution)/shard_map/while
  101.5 12.1 %copy-start.7 = (bf16[2048,6,64]{0,2,1:T(8,128)(2,1)S(1)}, bf16[2048,6,64]{0,2,1:T(8,128)(2,1)}, u32[]{:S(2)}) copy-start(bf16[2048,6,64]{0,2,1:T(8,128)(2,1)} %get-tuple-element.470) | copy-start | bytes 4718596 | tf_op jit(solution)/shard_map/while
  101.5 12.1 %copy-start.13 = (bf16[4,512,6,64]{1,3,2,0:T(8,128)(2,1)S(1)}, bf16[4,512,6,64]{1,3,2,0:T(8,128)(2,1)}, u32[]{:S(2)}) copy-start(bf16[4,512,6,64]{1,3,2,0:T(8,128)(2,1)} %get-tuple-element.455) | copy-start | bytes 4718596 | tf_op jit(solution)/shard_map/while
  141.3 12.1 %copy-start.7 = (bf16[2048,6,64]{0,2,1:T(8,128)(2,1)S(1)}, bf16[2048,6,64]{0,2,1:T(8,128)(2,1)}, u32[]{:S(2)}) copy-start(bf16[2048,6,64]{0,2,1:T(8,128)(2,1)} %get-tuple-element.470) | copy-start | bytes 4718596 | tf_op jit(solution)/shard_map/while
  141.3 12.1 %copy-start.13 = (bf16[4,512,6,64]{1,3,2,0:T(8,128)(2,1)S(1)}, bf16[4,512,6,64]{1,3,2,0:T(8,128)(2,1)}, u32[]{:S(2)}) copy-start(bf16[4,512,6,64]{1,3,2,0:T(8,128)(2,1)} %get-tuple-element.455) | copy-start | bytes 4718596 | tf_op jit(solution)/shard_map/while
  181.2 12.1 %copy-start.7 = (bf16[2048,6,64]{0,2,1:T(8,128)(2,1)S(1)}, bf16[2048,6,64]{0,2,1:T(8,128)(2,1)}, u32[]{:S(2)}) copy-start(bf16[2048,6,64]{0,2,1:T(8,128)(2,1)} %get-tuple-element.470) | copy-start | bytes 4718596 | tf_op jit(solution)/shard_map/while
  181.2 12.1 %copy-start.13 = (bf16[4,512,6,64]{1,3,2,0:T(8,128)(2,1)S(1)}, bf16[4,512,6,64]{1,3,2,0:T(8,128)(2,1)}, u32[]{:S(2)}) copy-start(bf16[4,512,6,64]{1,3,2,0:T(8,128)(2,1)} %get-tuple-element.455) | copy-start | bytes 4718596 | tf_op jit(solution)/shard_map/while
  214.1 12.3 %copy-start.21 = (f32[768]{0:T(1024)S(1)}, f32[768]{0:T(1024)}, u32[]{:S(2)}) copy-start(f32[768]{0:T(1024)} %get-tuple-element.249) | copy-start | bytes 9220
  214.2 68.3 %all-gather.7.cloned.1.call-start = ((), (), s32[]{:S(2)}) async-start(), calls=%async_computation.6 | async-start | bytes 4718592 | tf_op jit(solution)/shard_map/all_gather | solution.py:115
  232.2 50.3 %copy-start.48 = (f32[1536]{0:T(1024)S(1)}, f32[1536]{0:T(1024)}, u32[]{:S(2)}) copy-start(f32[1536]{0:T(1024)} %param.26) | copy-start | bytes 18436
  232.2 64.0 %all-gather.9.cloned.1.call-start = ((), (), s32[]{:S(2)}) async-start(), calls=%async_computation.8 | async-start | bytes 4718592 | tf_op jit(solution)/shard_map/all_gather | solution.py:128
  282.4 54.2 %reduce-scatter.9.cloned.1.call-start = ((), (), s32[]{:S(2)}) async-start(), calls=%async_computation.9 | async-start | bytes 4718592 | tf_op jit(solution)/shard_map/reduce_scatter | solution.py:139
  324.7 21.7 %reduce-scatter.7.cloned.1.call-start = ((), (), s32[]{:S(2)}) async-start(), calls=%async_computation.7 | async-start | bytes 4718592 | tf_op jit(solution)/shard_map/reduce_scatter | solution.py:120
  336.0 32.4 %all-gather.11.cloned.1.call-start = ((), (), s32[]{:S(2)}) async-start(), calls=%async_computation.10 | async-start | bytes 4718592 | tf_op jit(solution)/shard_map/all_gather | solution.py:149
  354.9 499.0 %reduce-scatter.11.cloned.1.call-start = ((), (), s32[]{:S(2)}) async-start(), calls=%async_computation.11 | async-start | bytes 4718592 | tf_op jit(solution)/shard_map/reduce_scatter | solution.py:210
  741.8 429.4 %all-reduce.5.cloned.1.call-start = ((), (), s32[]{:S(2)}) async-start(), calls=%async_computation.12 | async-start | bytes 28311552 | tf_op jit(solution)/shard_map/psum | solution.py:234
  741.9 9.8 copy-start.44
  751.7 9.1 copy-start.16
  751.7 9.1 copy-start.45
  770.3 83.7 %copy-start.6 = (bf16[1024,768]{1,0:T(8,128)(2,1)S(1)}, bf16[1024,768]{1,0:T(8,128)(2,1)}, u32[]{:S(2)}) copy-start(bf16[1024,768]{1,0:T(8,128)(2,1)} %param.16) | copy-start | bytes 4718596
  770.3 83.7 %copy-start.23 = (f32[1024]{0:T(1024)S(1)}, f32[1024]{0:T(1024)}, u32[]{:S(2)}) copy-start(f32[1024]{0:T(1024)} %copy-done.22) | copy-start | bytes 12292
  770.3 83.6 %copy-start.25 = (f32[768]{0:T(1024)S(1)}, f32[768]{0:T(1024)}, u32[]{:S(2)}) copy-start(f32[768]{0:T(1024)} %copy-done.24) | copy-start | bytes 9220
  770.3 86.3 %copy-start.30 = (f32[1024]{0:T(1024)S(1)}, f32[1024]{0:T(1024)}, u32[]{:S(2)}) copy-start(f32[1024]{0:T(1024)} %copy-done.29) | copy-start | bytes 12292
  770.3 86.3 %copy-start.28 = (f32[1024]{0:T(1024)S(1)}, f32[1024]{0:T(1024)}, u32[]{:S(2)}) copy-start(f32[1024]{0:T(1024)} %copy-done.27) | copy-start | bytes 12292
  1176.5 6.5 slice-start
  1177.5 7.7 copy-start.1
  (38 other events, 103.1 us)
Sparse Core Ops, SparseCore 0:
  15.0 14.8 all-gather.4
  214.3 12.0 reduce-scatter.4
  232.3 13.3 all-gather.6
  282.5 7.9 all-gather.8
  324.8 6.7 reduce-scatter.8
  336.1 10.2 reduce-scatter.6
  355.1 13.2 all-gather.10
  742.0 12.0 reduce-scatter.10
  770.5 400.7 all-reduce.4
where the time goes:
time: 1200 us; the launch traced here: 1190 us
  matrix products  448 us (37%)
  waiting for transfers between devices  308 us (26%)
  other arithmetic  188 us (16%)
  blocking collectives  165 us (14%)
  local copies, waits for them, and re-layouts  65.3 us (5%)
  between operations  15.9 us (1%)
    psum x1, waiting for transfers between devices, local(): lax.psum((grad_qkv, grad_qv_bias, grad_out, grad_fc1, grad_bfc1, grad_fc2...  267 us
    dot_general x8, matrix products, score_block(): jnp.einsum('qhd,khd->hqk', query_block, keys_all, preferred_element_type=...  101 us
    convert_element_type x4, other arithmetic, backward_block(): grad_scores = grad_scores.astype(jnp.bfloat16)  85.1 us
    psum x1, blocking collectives, local(): lax.psum((grad_qkv, grad_qv_bias, grad_out, grad_fc1, grad_bfc1, grad_fc2...  81.2 us
    dot_general x4, matrix products, backward_block(): jnp.einsum('qhd,khd->hqk', grad_block, values_all, preferred_element_type...  72.3 us
    dot_general x4, matrix products, backward_block(): jnp.einsum('hqk,qhd->khd', probs.astype(jnp.bfloat16), grad_block, prefer...  53.8 us
    reduce_sum x4, other arithmetic, forward_block(): total = jnp.sum(exponent, axis=-1, keepdims=True)  48.4 us
    dot_general x4, matrix products, forward_block(): jnp.einsum('hqk,khd->qhd', weights, values_all, preferred_element_type=jn...  46.6 us
  transfers between devices with their start and end apart: 9, of which 5 were waited for; matrix products, arithmetic and copies ran while one was open for 6% of the time, Pallas kernels for 0%

commit v1 on v0

--- a/solution.py
+++ b/solution.py
@@ -218,18 +218,21 @@
     grad_input, grad_gain_one, grad_shift_one = norm_pull(grad_norm_one)
     grad_input = grad_input + grad_hidden
     gain_grads, shift_grads = lax.psum(
-        (
-            jnp.stack([grad_gain_one, grad_gain_two]),
-            jnp.stack(
-                [
-                    grad_shift_one,
-                    grad_shift_two,
-                    jnp.sum(grad_hidden, axis=0),
-                    jnp.sum(out_cot, axis=0),
-                ]
+        lax.psum(
+            (
+                jnp.stack([grad_gain_one, grad_gain_two]),
+                jnp.stack(
+                    [
+                        grad_shift_one,
+                        grad_shift_two,
+                        jnp.sum(grad_hidden, axis=0),
+                        jnp.sum(out_cot, axis=0),
+                    ]
+                ),
             ),
-        ),
-        ("dp", "mp"),
+            "mp",
+        ),
+        "dp",
     )
     grad_qkv, grad_qv_bias, grad_out, grad_fc1, grad_bfc1, grad_fc2 = lax.psum(
         (grad_qkv, grad_qv_bias, grad_out, grad_fc1, grad_bfc1, grad_fc2), "dp"

time: 1200 us -> 1200 us (level)
  blocking collectives: 165 us -> 127 us
  waiting for transfers between devices: 308 us -> 344 us
    psum x1, blocking collectives: 41.5 us -> 3.43 us  [local(): lax.psum((jnp.stack([grad_gain_one, grad_gain_two]), jnp.stack([grad_shif...]
    psum x1, waiting for transfers between devices: 267 us -> 303 us  [local(): lax.psum((grad_qkv, grad_qv_bias, grad_out, grad_fc1, grad_bfc1, grad_fc2...]
where the time goes in v1:
time: 1200 us; the launch traced here: 1190 us
  matrix products  448 us (37%)
  waiting for transfers between devices  344 us (29%)
  other arithmetic  188 us (16%)
  blocking collectives  127 us (11%)
  local copies, waits for them, and re-layouts  65.3 us (5%)
  between operations  16 us (1%)
    psum x1, waiting for transfers between devices, local(): lax.psum((grad_qkv, grad_qv_bias, grad_out, grad_fc1, grad_bfc1, grad_fc2...  303 us
    dot_general x8, matrix products, score_block(): jnp.einsum('qhd,khd->hqk', query_block, keys_all, preferred_element_type=...  101 us
    convert_element_type x4, other arithmetic, backward_block(): grad_scores = grad_scores.astype(jnp.bfloat16)  85.1 us
    psum x1, blocking collectives, local(): lax.psum(lax.psum((jnp.stack([grad_gain_one, grad_gain_two]), jnp.stack([...  81.8 us
    dot_general x4, matrix products, backward_block(): jnp.einsum('qhd,khd->hqk', grad_block, values_all, preferred_element_type...  72.3 us
    dot_general x4, matrix products, backward_block(): jnp.einsum('hqk,qhd->khd', probs.astype(jnp.bfloat16), grad_block, prefer...  53.8 us
    reduce_sum x4, other arithmetic, forward_block(): total = jnp.sum(exponent, axis=-1, keepdims=True)  48.4 us
    dot_general x4, matrix products, forward_block(): jnp.einsum('hqk,khd->qhd', weights, values_all, preferred_element_type=jn...  46.6 us
  transfers between devices with their start and end apart: 9, of which 5 were waited for; matrix products, arithmetic and copies ran while one was open for 6% of the time, Pallas kernels for 0%

profile of v1, /device:TPU:0, one launch (start us, length us, event | category | flops | bytes accessed | tf_op | source)
XLA Modules:
  0.0 1190.8 jit_solution(8026270459712380475)
XLA Ops:
  15.6 14.2 %all-gather.5.cloned.1.call-done = bf16[2048,768]{1,0:T(8,128)(2,1)} async-done(((bf16[1024,768]{1,0:T(8,128)(2,1)}), bf16[2048,768]{1,0:T(8,128)(2,1)}) %all-gather.5.cloned.1.call-update) | async-done | bytes 3145744 | tf_op jit(solution)/shard_map/all_gather | solution.py:78
  46.7 159.6 %while.27 = (s32[]{:T(128)}, bf16[4,512,6,64]{1,3,2,0:T(8,128)(2,1)}, f32[4,6,512]{2,1,0:T(8,128)S(1)}, s32[4,512]{1,0:T(4,128)S(1)}, s32[2048]{0:T(1024)S(1)}, ...) while((s32[]{:T(128)}, ...), condition=%wide.region_7.8_spmd, body=%wide.region_4.7_spmd.sunk | while | flops 1687155712 | bytes 103024832 | solution.py:104
  47.3 14.3 %fusion.128 = (f32[6,512]{1,0:T(8,128)S(1)}, f32[6,512,2048]{2,1,0:T(8,128)}) fusion(pred[512,2048]{1,0:T(8,128)(4,1)S(1)} %broadcast_compare_fusion.4, bf16[2048,6,64]{0,2,1:T(8,128)(2,1)} %get-tuple-element.471, bf16[4,512,6,64]{1,3,2,0:T(8,128)(2,1)} %get-tuple-element.470, s32[]{:T(128)S(6)} %copy.67), kind=kOutput, calls=%fused_computation.3.clone.1 | convolution fusion | flops 824177664 | bytes 28192772 | tf_op jit(solution)/shard_map/while/body/eval_jaxpr/qhd,khd->hqk/dot_general | solution.py:38
  61.6 12.1 %fusion.129 = f32[6,512]{1,0:T(8,128)S(1)} fusion(f32[6,512,2048]{2,1,0:T(8,128)} %get-tuple-element.432, f32[6,512]{1,0:T(8,128)S(1)} %get-tuple-element.433, pred[512,2048]{1,0:T(8,128)(4,1)S(1)} %broadcast_compare_fusion.4), kind=kLoop, calls=%fused_computation.4.clone.1 | loop fusion | flops 25162752 | bytes 26238976 | tf_op jit(solution)/shard_map/while/body/eval_jaxpr/reduce_sum | solution.py:97
  87.2 14.3 %fusion.128 = (f32[6,512]{1,0:T(8,128)S(1)}, f32[6,512,2048]{2,1,0:T(8,128)}) fusion(pred[512,2048]{1,0:T(8,128)(4,1)S(1)} %broadcast_compare_fusion.4, bf16[2048,6,64]{0,2,1:T(8,128)(2,1)} %get-tuple-element.471, bf16[4,512,6,64]{1,3,2,0:T(8,128)(2,1)} %get-tuple-element.470, s32[]{:T(128)S(6)} %copy.67), kind=kOutput, calls=%fused_computation.3.clone.1 | convolution fusion | flops 824177664 | bytes 28192772 | tf_op jit(solution)/shard_map/while/body/eval_jaxpr/qhd,khd->hqk/dot_general | solution.py:38
  101.5 12.1 %fusion.129 = f32[6,512]{1,0:T(8,128)S(1)} fusion(f32[6,512,2048]{2,1,0:T(8,128)} %get-tuple-element.432, f32[6,512]{1,0:T(8,128)S(1)} %get-tuple-element.433, pred[512,2048]{1,0:T(8,128)(4,1)S(1)} %broadcast_compare_fusion.4), kind=kLoop, calls=%fused_computation.4.clone.1 | loop fusion | flops 25162752 | bytes 26238976 | tf_op jit(solution)/shard_map/while/body/eval_jaxpr/reduce_sum | solution.py:97
  113.6 11.6 fusion.130
  127.1 14.3 %fusion.128 = (f32[6,512]{1,0:T(8,128)S(1)}, f32[6,512,2048]{2,1,0:T(8,128)}) fusion(pred[512,2048]{1,0:T(8,128)(4,1)S(1)} %broadcast_compare_fusion.4, bf16[2048,6,64]{0,2,1:T(8,128)(2,1)} %get-tuple-element.471, bf16[4,512,6,64]{1,3,2,0:T(8,128)(2,1)} %get-tuple-element.470, s32[]{:T(128)S(6)} %copy.67), kind=kOutput, calls=%fused_computation.3.clone.1 | convolution fusion | flops 824177664 | bytes 28192772 | tf_op jit(solution)/shard_map/while/body/eval_jaxpr/qhd,khd->hqk/dot_general | solution.py:38
  141.3 12.1 %fusion.129 = f32[6,512]{1,0:T(8,128)S(1)} fusion(f32[6,512,2048]{2,1,0:T(8,128)} %get-tuple-element.432, f32[6,512]{1,0:T(8,128)S(1)} %get-tuple-element.433, pred[512,2048]{1,0:T(8,128)(4,1)S(1)} %broadcast_compare_fusion.4), kind=kLoop, calls=%fused_computation.4.clone.1 | loop fusion | flops 25162752 | bytes 26238976 | tf_op jit(solution)/shard_map/while/body/eval_jaxpr/reduce_sum | solution.py:97
  166.9 14.3 %fusion.128 = (f32[6,512]{1,0:T(8,128)S(1)}, f32[6,512,2048]{2,1,0:T(8,128)}) fusion(pred[512,2048]{1,0:T(8,128)(4,1)S(1)} %broadcast_compare_fusion.4, bf16[2048,6,64]{0,2,1:T(8,128)(2,1)} %get-tuple-element.471, bf16[4,512,6,64]{1,3,2,0:T(8,128)(2,1)} %get-tuple-element.470, s32[]{:T(128)S(6)} %copy.67), kind=kOutput, calls=%fused_computation.3.clone.1 | convolution fusion | flops 824177664 | bytes 28192772 | tf_op jit(solution)/shard_map/while/body/eval_jaxpr/qhd,khd->hqk/dot_general | solution.py:38
  181.2 12.1 %fusion.129 = f32[6,512]{1,0:T(8,128)S(1)} fusion(f32[6,512,2048]{2,1,0:T(8,128)} %get-tuple-element.432, f32[6,512]{1,0:T(8,128)S(1)} %get-tuple-element.433, pred[512,2048]{1,0:T(8,128)(4,1)S(1)} %broadcast_compare_fusion.4), kind=kLoop, calls=%fused_computation.4.clone.1 | loop fusion | flops 25162752 | bytes 26238976 | tf_op jit(solution)/shard_map/while/body/eval_jaxpr/reduce_sum | solution.py:97
  193.3 11.6 fusion.130
  214.2 12.2 %reduce-scatter.5.cloned.1.call-done = bf16[1024,768]{1,0:T(8,128)(2,1)} async-done(((bf16[2048,768]{1,0:T(8,128)(2,1)}), bf16[1024,768]{1,0:T(8,128)(2,1)}) %reduce-scatter.5.cloned.1.call-update) | async-done | bytes 1572880 | tf_op jit(solution)/shard_map/reduce_scatter | solution.py:107
  234.2 41.9 %psum.77 = f32[3]{0:T(128)S(1)} all-reduce(f32[3]{0:T(128)S(1)} %compare_select_fusion.1), channel_id=1, replica_groups=mesh['dp'=16,'mp'=2] {'dp'}, use_global_device_ids=true, to_apply=%region_14.15 | all-reduce | flops 3 | bytes 24 | tf_op jit(solution)/shard_map/psum | solution.py:64
  282.4 13.7 %multiply_convert_fusion.1 = (bf16[2048,1536]{1,0:T(8,128)(2,1)}, f32[2048,1536]{1,0:T(8,128)}) fusion(f32[1536]{0:T(1024)S(1)} %copy-done.48, bf16[2048,768]{1,0:T(8,128)(2,1)} %all-gather.7.cloned.1.call-done, bf16[768,1536]{1,0:T(8,128)(2,1)S(1)} %copy-done), kind=kOutput, calls=%fused_computation.58 | convolution fusion | flops 4863295488 | bytes 24385536 | tf_op jit(solution)/shard_map/dot_general | solution.py:116
  296.1 19.5 %convert_reduce_fusion = (f32[1536]{0:T(1024)}, bf16[2048,1536]{1,0:T(8,128)(2,1)S(1)}) fusion(bf16[2048,768]{1,0:T(8,128)(2,1)} %all-gather.9.cloned.1.call-done, bf16[1536,768]{1,0:T(8,128)(2,1)} %param.27, f32[2048,1536]{1,0:T(8,128)} %get-tuple-element.320, f32[1536]{0:T(1024)S(1)} %copy-done.48), kind=kOutput, calls=%fused_computation.57 | convolution fusion | flops 4916771328 | bytes 24391680 | tf_op jit(solution)/shard_map/rd,fd->rf/dot_general | solution.py:132
  355.0 13.4 %all-gather.11.cloned.1.call-done = bf16[2048,768]{1,0:T(8,128)(2,1)} async-done(((bf16[1024,768]{1,0:T(8,128)(2,1)}), bf16[2048,768]{1,0:T(8,128)(2,1)}) %all-gather.11.cloned.1.call-update) | async-done | bytes 3145744 | tf_op jit(solution)/shard_map/all_gather | solution.py:149
  381.7 333.3 %while.28 = (s32[]{:T(128)}, f32[2048,6,64]{0,2,1:T(8,128)}, f32[2048,6,64]{0,2,1:T(8,128)}, bf16[4,512,6,64]{1,3,2,0:T(8,128)(2,1)}, bf16[4,512,6,64]{1,3,2,0:T...) while((s32[]{:T(128)}, f32[2048,6,64]{0,2,1:T(8,128)}, ...), condition=%wide.region_23.24_spmd.clone, body=%wide.region_21.23_spmd.clone.sunk | while | flops 4126077952 | bytes 212699312 | solution.py:188
  393.7 12.8 %bitcast_add_fusion.5 = f32[2048,6,64]{0,2,1:T(8,128)} fusion(f32[2048,6,64]{0,2,1:T(8,128)} %get-tuple-element.489, f32[6,512,2048]{2,1,0:T(8,128)} %fusion.140, f32[6,512]{1,0:T(8,128)S(1)} %dynamic-slice_bitcast_fusion.2, pred[512,2048]{1,0:T(8,128)(4,1)S(1)} %broadcast_compare_fusion.5, pred[]{:T(512)S(6)} %compare.3, ...), kind=kOutput, calls=%fused_computation.23.clone.1 | convolution fusion | flops 832045056 | bytes 32911364 | tf_op jit(solution)/shard_map/while/body/eval_jaxpr/hqk,qhd->khd/dot_general | solution.py:163
  406.5 18.1 %multiply_reduce_fusion.3 = (f32[6,512]{1,0:T(8,128)S(1)}, f32[6,512,2048]{2,1,0:T(8,128)}) fusion(f32[6,512,2048]{2,1,0:T(8,128)} %fusion.140, f32[6,512]{1,0:T(8,128)S(1)} %dynamic-slice_bitcast_fusion.2, pred[512,2048]{1,0:T(8,128)(4,1)S(1)} %broadcast_compare_fusion.5, bf16[2048,6,64]{0,2,1:T(8,128)(2,1)} %get-tuple-element.510, ...), kind=kOutput, calls=%fused_computation.18.clone.1 | convolution fusion | flops 836760576 | bytes 53370884 | tf_op jit(solution)/shard_map/while/body/eval_jaxpr/qhd,khd->hqk/dot_general | solution.py:169
  424.6 21.3 %multiply_convert_fusion.3 = bf16[6,512,2048]{2,1,0:T(8,128)(2,1)} fusion(f32[6,512,2048]{2,1,0:T(8,128)} %get-tuple-element.445, f32[6,512,2048]{2,1,0:T(8,128)} %fusion.140, f32[6,512]{1,0:T(8,128)S(1)} %get-tuple-element.446, f32[6,512]{1,0:T(8,128)S(1)} %dynamic-slice_bitcast_fusion.2, pred[512,2048]{1,0:T(8,128)(4,1)S(1)} %broadcast_compare_fusion.5), kind=kLoop, calls=%fused_computation.17.clone.1 | loop fusion | flops 37748736 | bytes 63987712 | tf_op jit(solution)/shard_map/while/body/eval_jaxpr/convert_element_type | solution.py:173
  475.5 13.7 %bitcast_add_fusion.5 = f32[2048,6,64]{0,2,1:T(8,128)} fusion(f32[2048,6,64]{0,2,1:T(8,128)} %get-tuple-element.489, f32[6,512,2048]{2,1,0:T(8,128)} %fusion.140, f32[6,512]{1,0:T(8,128)S(1)} %dynamic-slice_bitcast_fusion.2, pred[512,2048]{1,0:T(8,128)(4,1)S(1)} %broadcast_compare_fusion.5, pred[]{:T(512)S(6)} %compare.3, ...), kind=kOutput, calls=%fused_computation.23.clone.1 | convolution fusion | flops 832045056 | bytes 32911364 | tf_op jit(solution)/shard_map/while/body/eval_jaxpr/hqk,qhd->khd/dot_general | solution.py:163
  489.2 18.1 %multiply_reduce_fusion.3 = (f32[6,512]{1,0:T(8,128)S(1)}, f32[6,512,2048]{2,1,0:T(8,128)}) fusion(f32[6,512,2048]{2,1,0:T(8,128)} %fusion.140, f32[6,512]{1,0:T(8,128)S(1)} %dynamic-slice_bitcast_fusion.2, pred[512,2048]{1,0:T(8,128)(4,1)S(1)} %broadcast_compare_fusion.5, bf16[2048,6,64]{0,2,1:T(8,128)(2,1)} %get-tuple-element.510, ...), kind=kOutput, calls=%fused_computation.18.clone.1 | convolution fusion | flops 836760576 | bytes 53370884 | tf_op jit(solution)/shard_map/while/body/eval_jaxpr/qhd,khd->hqk/dot_general | solution.py:169
  507.3 21.3 %multiply_convert_fusion.3 = bf16[6,512,2048]{2,1,0:T(8,128)(2,1)} fusion(f32[6,512,2048]{2,1,0:T(8,128)} %get-tuple-element.445, f32[6,512,2048]{2,1,0:T(8,128)} %fusion.140, f32[6,512]{1,0:T(8,128)S(1)} %get-tuple-element.446, f32[6,512]{1,0:T(8,128)S(1)} %dynamic-slice_bitcast_fusion.2, pred[512,2048]{1,0:T(8,128)(4,1)S(1)} %broadcast_compare_fusion.5), kind=kLoop, calls=%fused_computation.17.clone.1 | loop fusion | flops 37748736 | bytes 63987712 | tf_op jit(solution)/shard_map/while/body/eval_jaxpr/convert_element_type | solution.py:173
  559.1 13.7 %bitcast_add_fusion.5 = f32[2048,6,64]{0,2,1:T(8,128)} fusion(f32[2048,6,64]{0,2,1:T(8,128)} %get-tuple-element.489, f32[6,512,2048]{2,1,0:T(8,128)} %fusion.140, f32[6,512]{1,0:T(8,128)S(1)} %dynamic-slice_bitcast_fusion.2, pred[512,2048]{1,0:T(8,128)(4,1)S(1)} %broadcast_compare_fusion.5, pred[]{:T(512)S(6)} %compare.3, ...), kind=kOutput, calls=%fused_computation.23.clone.1 | convolution fusion | flops 832045056 | bytes 32911364 | tf_op jit(solution)/shard_map/while/body/eval_jaxpr/hqk,qhd->khd/dot_general | solution.py:163
  572.8 18.1 %multiply_reduce_fusion.3 = (f32[6,512]{1,0:T(8,128)S(1)}, f32[6,512,2048]{2,1,0:T(8,128)}) fusion(f32[6,512,2048]{2,1,0:T(8,128)} %fusion.140, f32[6,512]{1,0:T(8,128)S(1)} %dynamic-slice_bitcast_fusion.2, pred[512,2048]{1,0:T(8,128)(4,1)S(1)} %broadcast_compare_fusion.5, bf16[2048,6,64]{0,2,1:T(8,128)(2,1)} %get-tuple-element.510, ...), kind=kOutput, calls=%fused_computation.18.clone.1 | convolution fusion | flops 836760576 | bytes 53370884 | tf_op jit(solution)/shard_map/while/body/eval_jaxpr/qhd,khd->hqk/dot_general | solution.py:169
  590.9 21.3 %multiply_convert_fusion.3 = bf16[6,512,2048]{2,1,0:T(8,128)(2,1)} fusion(f32[6,512,2048]{2,1,0:T(8,128)} %get-tuple-element.445, f32[6,512,2048]{2,1,0:T(8,128)} %fusion.140, f32[6,512]{1,0:T(8,128)S(1)} %get-tuple-element.446, f32[6,512]{1,0:T(8,128)S(1)} %dynamic-slice_bitcast_fusion.2, pred[512,2048]{1,0:T(8,128)(4,1)S(1)} %broadcast_compare_fusion.5), kind=kLoop, calls=%fused_computation.17.clone.1 | loop fusion | flops 37748736 | bytes 63987712 | tf_op jit(solution)/shard_map/while/body/eval_jaxpr/convert_element_type | solution.py:173
  642.7 13.7 %bitcast_add_fusion.5 = f32[2048,6,64]{0,2,1:T(8,128)} fusion(f32[2048,6,64]{0,2,1:T(8,128)} %get-tuple-element.489, f32[6,512,2048]{2,1,0:T(8,128)} %fusion.140, f32[6,512]{1,0:T(8,128)S(1)} %dynamic-slice_bitcast_fusion.2, pred[512,2048]{1,0:T(8,128)(4,1)S(1)} %broadcast_compare_fusion.5, pred[]{:T(512)S(6)} %compare.3, ...), kind=kOutput, calls=%fused_computation.23.clone.1 | convolution fusion | flops 832045056 | bytes 32911364 | tf_op jit(solution)/shard_map/while/body/eval_jaxpr/hqk,qhd->khd/dot_general | solution.py:163
  656.4 18.1 %multiply_reduce_fusion.3 = (f32[6,512]{1,0:T(8,128)S(1)}, f32[6,512,2048]{2,1,0:T(8,128)}) fusion(f32[6,512,2048]{2,1,0:T(8,128)} %fusion.140, f32[6,512]{1,0:T(8,128)S(1)} %dynamic-slice_bitcast_fusion.2, pred[512,2048]{1,0:T(8,128)(4,1)S(1)} %broadcast_compare_fusion.5, bf16[2048,6,64]{0,2,1:T(8,128)(2,1)} %get-tuple-element.510, ...), kind=kOutput, calls=%fused_computation.18.clone.1 | convolution fusion | flops 836760576 | bytes 53370884 | tf_op jit(solution)/shard_map/while/body/eval_jaxpr/qhd,khd->hqk/dot_general | solution.py:169
  674.5 21.3 %multiply_convert_fusion.3 = bf16[6,512,2048]{2,1,0:T(8,128)(2,1)} fusion(f32[6,512,2048]{2,1,0:T(8,128)} %get-tuple-element.445, f32[6,512,2048]{2,1,0:T(8,128)} %fusion.140, f32[6,512]{1,0:T(8,128)S(1)} %get-tuple-element.446, f32[6,512]{1,0:T(8,128)S(1)} %dynamic-slice_bitcast_fusion.2, pred[512,2048]{1,0:T(8,128)(4,1)S(1)} %broadcast_compare_fusion.5), kind=kLoop, calls=%fused_computation.17.clone.1 | loop fusion | flops 37748736 | bytes 63987712 | tf_op jit(solution)/shard_map/while/body/eval_jaxpr/convert_element_type | solution.py:173
  781.1 81.8 %all-reduce = (f32[2,768]{1,0:T(2,128)}, f32[4,768]{1,0:T(4,128)}, f32[2,384]{1,0:T(2,128)}, f32[1536]{0:T(1024)}) all-reduce(f32[2,768]{1,0:T(2,128)S(1)} %get-tuple-element.302, f32[4,768]{1,0:T(4,128)S(1)} %get-tuple-element.303, f32[2,384]{1,0:T(2,128)S(1)} %pad_maximum_fusion.6, ...), channel_id=1, replica_groups=mesh['dp'=16,'mp'=2] {'dp'}, use_global_device_ids=true, to_apply=%region_30.31 | all-reduce | flops 6912 | bytes 55296 | tf_op jit(solution)/shard_map/psum | solution.py:220
  867.0 303.1 %all-reduce.5.cloned.1.call-done = (f32[3,768,384]{1,2,0:T(8,128)}, f32[384,768]{1,0:T(8,128)}, f32[768,1536]{1,0:T(8,128)}, f32[1536,768]{1,0:T(8,128)}) async-done(((f32[3,768,384]{1,2,0:T(8,128)}, f32[384,768]{1,0:T(8,128)}, f32[768,1536]{1,0:T(8,128)}, f32[1536,768]{1,0:T(8,128)}), (f32[3,768,384]{1,2,0:T(8,128)}, f32[384,768]{1,0:T(8,128)}, f32[768,1536]{1,0:T(8,128)}, ...) | async-done | bytes 14155792 | tf_op jit(solution)/shard_map/psum | solution.py:237
  (269 shorter events, 334.1 us)
Async XLA Ops:
  7.2 275.3 %copy-start = (bf16[768,1536]{1,0:T(8,128)(2,1)S(1)}, bf16[768,1536]{1,0:T(8,128)(2,1)}, u32[]{:S(2)}) copy-start(bf16[768,1536]{1,0:T(8,128)(2,1)} %param.25) | copy-start | bytes 7077892
  7.2 5.2 copy-start.37
  7.2 22.6 %all-gather.5.cloned.1.call-start = ((), (), s32[]{:S(2)}) async-start(), calls=%async_computation.4 | async-start | bytes 4718592 | tf_op jit(solution)/shard_map/all_gather | solution.py:78
  7.3 5.8 copy-start.3
  9.1 5.8 copy-start.41
  9.1 6.3 copy-start.40
  14.8 211.6 %reduce-scatter.5.cloned.1.call-start = ((), (), s32[]{:S(2)}) async-start(), calls=%async_computation.5 | async-start | bytes 4718592 | tf_op jit(solution)/shard_map/reduce_scatter | solution.py:107
  61.6 12.1 %copy-start.7 = (bf16[2048,6,64]{0,2,1:T(8,128)(2,1)S(1)}, bf16[2048,6,64]{0,2,1:T(8,128)(2,1)}, u32[]{:S(2)}) copy-start(bf16[2048,6,64]{0,2,1:T(8,128)(2,1)} %get-tuple-element.472) | copy-start | bytes 4718596 | tf_op jit(solution)/shard_map/while
  61.6 12.1 %copy-start.13 = (bf16[4,512,6,64]{1,3,2,0:T(8,128)(2,1)S(1)}, bf16[4,512,6,64]{1,3,2,0:T(8,128)(2,1)}, u32[]{:S(2)}) copy-start(bf16[4,512,6,64]{1,3,2,0:T(8,128)(2,1)} %get-tuple-element.457) | copy-start | bytes 4718596 | tf_op jit(solution)/shard_map/while
  101.5 12.1 %copy-start.7 = (bf16[2048,6,64]{0,2,1:T(8,128)(2,1)S(1)}, bf16[2048,6,64]{0,2,1:T(8,128)(2,1)}, u32[]{:S(2)}) copy-start(bf16[2048,6,64]{0,2,1:T(8,128)(2,1)} %get-tuple-element.472) | copy-start | bytes 4718596 | tf_op jit(solution)/shard_map/while
  101.5 12.1 %copy-start.13 = (bf16[4,512,6,64]{1,3,2,0:T(8,128)(2,1)S(1)}, bf16[4,512,6,64]{1,3,2,0:T(8,128)(2,1)}, u32[]{:S(2)}) copy-start(bf16[4,512,6,64]{1,3,2,0:T(8,128)(2,1)} %get-tuple-element.457) | copy-start | bytes 4718596 | tf_op jit(solution)/shard_map/while
  141.3 12.1 %copy-start.7 = (bf16[2048,6,64]{0,2,1:T(8,128)(2,1)S(1)}, bf16[2048,6,64]{0,2,1:T(8,128)(2,1)}, u32[]{:S(2)}) copy-start(bf16[2048,6,64]{0,2,1:T(8,128)(2,1)} %get-tuple-element.472) | copy-start | bytes 4718596 | tf_op jit(solution)/shard_map/while
  141.3 12.1 %copy-start.13 = (bf16[4,512,6,64]{1,3,2,0:T(8,128)(2,1)S(1)}, bf16[4,512,6,64]{1,3,2,0:T(8,128)(2,1)}, u32[]{:S(2)}) copy-start(bf16[4,512,6,64]{1,3,2,0:T(8,128)(2,1)} %get-tuple-element.457) | copy-start | bytes 4718596 | tf_op jit(solution)/shard_map/while
  181.2 12.1 %copy-start.7 = (bf16[2048,6,64]{0,2,1:T(8,128)(2,1)S(1)}, bf16[2048,6,64]{0,2,1:T(8,128)(2,1)}, u32[]{:S(2)}) copy-start(bf16[2048,6,64]{0,2,1:T(8,128)(2,1)} %get-tuple-element.472) | copy-start | bytes 4718596 | tf_op jit(solution)/shard_map/while
  181.2 12.1 %copy-start.13 = (bf16[4,512,6,64]{1,3,2,0:T(8,128)(2,1)S(1)}, bf16[4,512,6,64]{1,3,2,0:T(8,128)(2,1)}, u32[]{:S(2)}) copy-start(bf16[4,512,6,64]{1,3,2,0:T(8,128)(2,1)} %get-tuple-element.457) | copy-start | bytes 4718596 | tf_op jit(solution)/shard_map/while
  214.1 12.3 %copy-start.21 = (f32[768]{0:T(1024)S(1)}, f32[768]{0:T(1024)}, u32[]{:S(2)}) copy-start(f32[768]{0:T(1024)} %get-tuple-element.249) | copy-start | bytes 9220
  214.2 68.3 %all-gather.7.cloned.1.call-start = ((), (), s32[]{:S(2)}) async-start(), calls=%async_computation.6 | async-start | bytes 4718592 | tf_op jit(solution)/shard_map/all_gather | solution.py:115
  232.2 50.3 %copy-start.48 = (f32[1536]{0:T(1024)S(1)}, f32[1536]{0:T(1024)}, u32[]{:S(2)}) copy-start(f32[1536]{0:T(1024)} %param.26) | copy-start | bytes 18436
  232.2 64.0 %all-gather.9.cloned.1.call-start = ((), (), s32[]{:S(2)}) async-start(), calls=%async_computation.8 | async-start | bytes 4718592 | tf_op jit(solution)/shard_map/all_gather | solution.py:128
  282.4 54.2 %reduce-scatter.9.cloned.1.call-start = ((), (), s32[]{:S(2)}) async-start(), calls=%async_computation.9 | async-start | bytes 4718592 | tf_op jit(solution)/shard_map/reduce_scatter | solution.py:139
  324.7 21.7 %reduce-scatter.7.cloned.1.call-start = ((), (), s32[]{:S(2)}) async-start(), calls=%async_computation.7 | async-start | bytes 4718592 | tf_op jit(solution)/shard_map/reduce_scatter | solution.py:120
  336.0 32.4 %all-gather.11.cloned.1.call-start = ((), (), s32[]{:S(2)}) async-start(), calls=%async_computation.10 | async-start | bytes 4718592 | tf_op jit(solution)/shard_map/all_gather | solution.py:149
  354.9 417.8 %reduce-scatter.11.cloned.1.call-start = ((), (), s32[]{:S(2)}) async-start(), calls=%async_computation.11 | async-start | bytes 4718592 | tf_op jit(solution)/shard_map/reduce_scatter | solution.py:210
  741.8 428.3 %all-reduce.5.cloned.1.call-start = ((), (), s32[]{:S(2)}) async-start(), calls=%async_computation.12 | async-start | bytes 28311552 | tf_op jit(solution)/shard_map/psum | solution.py:237
  741.9 9.8 copy-start.44
  751.7 9.1 copy-start.16
  751.7 9.1 copy-start.45
  772.7 8.4 copy-start.38
  1170.1 5.3 copy-start.20
  1175.4 6.5 slice-start
  1176.4 5.5 slice-start.1
  1176.4 7.7 copy-start.1
  (38 other events, 96.6 us)
Sparse Core Ops, SparseCore 0:
  15.0 14.8 all-gather.4
  214.3 12.0 reduce-scatter.4
  232.3 13.3 all-gather.6
  282.5 7.9 all-gather.8
  324.8 6.7 reduce-scatter.8
  336.1 10.2 reduce-scatter.6
  355.1 13.2 all-gather.10
  742.0 12.0 reduce-scatter.10
  770.4 399.6 all-reduce.4
